TPU v7x, 256 devices: a whole 4x4x8 slice. The times are simulated.
256 devices in a mesh: outer: 8 (over z), inner: 32 (over y, x, core).
Axes of the slice: x: 4, y: 4, z: 8, core: 2. Of those that a mesh axis runs over, the one named last changes fastest.
Arguments:
- context: bfloat16 [32768, 4096], P(('outer', 'inner')), may hold values from -5 to 5
- query_acts: bfloat16 [64, 4096], replicated, may hold values from -5 to 5
- norm_gain: float32 [4096], replicated, may hold values from 0.25 to 1.75
- w_query: bfloat16 [4096, 2048], P('inner'), may hold values from -0.078125 to 0.078125
- w_key: bfloat16 [4096, 512], P('inner'), may hold values from -0.453125 to 0.453125
- value_weight: bfloat16 [4096, 512], P('inner'), may hold values from -0.09375 to 0.09375
- lengths: int32 [256], replicated, may hold values from 64 to 128, as said below
Outputs:
- block_out: bfloat16 [32768, 2048], P(('outer', 'inner'))
- query_out: bfloat16 [64, 2048], replicated
Inputs may be any that keep to these rules, and one draw needn't show every extreme that they name: `lengths`: valid tokens of a block are its first ones; the rest of it is padding.
All inputs are finite; a program needn't handle non-finite values.
Results may differ from a plain program's by a relative error of at most 0.004.
The roundings to bfloat16 on the way count: a program that leaves them out, or rounds other values in their place, can miss the bound.
Values may be sent and summed in bfloat16 or wider, within the bound.
No kernel may reach another device: no remote copies, remote signals or barrier semaphores. Data moves between devices by JAX's collectives and lax.ppermute only.
A program may use at most 320 MiB of HBM per device.

v0:
```python
import jax
import jax.numpy as jnp
from jax import lax
from jax.sharding import PartitionSpec as P

QUERY_HEADS = 16
KEY_VALUE_HEADS = 4
HEAD_SIZE = 128
epsilon = 1e-05


def broadcast(block, axis, owner):
    block = jnp.where(lax.axis_index(axis) == owner, block, jnp.zeros_like(block))
    return lax.psum(block, axis)


def normalize(matrix, norm_gain):
    widened = matrix.astype(jnp.float32)
    factor = lax.rsqrt(jnp.mean(widened * widened, axis=-1, keepdims=True) + epsilon)
    return (widened * factor * norm_gain).astype(jnp.bfloat16)


def attend_part(query_rows, key_row_block, value_matrix, allowed):
    count_of_rows = query_rows.shape[0]
    head_groups = query_rows.reshape(
        count_of_rows, KEY_VALUE_HEADS, QUERY_HEADS // KEY_VALUE_HEADS, HEAD_SIZE
    )
    per_head_keys = key_row_block.reshape(key_row_block.shape[0], KEY_VALUE_HEADS, HEAD_SIZE)
    per_head_values = value_matrix.reshape(value_matrix.shape[0], KEY_VALUE_HEADS, HEAD_SIZE)
    scores = jnp.einsum(
        "rhgd,khd->hgrk", head_groups, per_head_keys, preferred_element_type=jnp.float32
    ) * HEAD_SIZE ** (-0.5)
    scores = jnp.where(allowed, scores, -jnp.inf)
    maxima = jnp.max(scores, axis=-1)
    weights = jnp.exp(scores - maxima[..., None])
    sum_exp = jnp.sum(weights, axis=-1)
    numerator = jnp.einsum(
        "hgrk,khd->rhgd",
        weights.astype(jnp.bfloat16),
        per_head_values,
        preferred_element_type=jnp.float32,
    )
    return (
        maxima.reshape(QUERY_HEADS, count_of_rows),
        sum_exp.reshape(QUERY_HEADS, count_of_rows),
        numerator.reshape(count_of_rows, QUERY_HEADS * HEAD_SIZE),
    )


def spread(factor):
    return jnp.repeat(factor.T, HEAD_SIZE, axis=1)


def combine(former, latter):
    maxima = jnp.maximum(former[0], latter[0])
    scale_one = jnp.exp(former[0] - maxima)
    scale_two = jnp.exp(latter[0] - maxima)
    return (
        maxima,
        former[1] * scale_one + latter[1] * scale_two,
        former[2] * spread(scale_one) + latter[2] * spread(scale_two),
    )


def finish(pieces):
    return (pieces[2] / spread(pieces[1])).astype(jnp.bfloat16)


def share_anchor(stacked):
    return broadcast(stacked, ("outer", "inner"), 0)


def per_device(context, query_acts, norm_gain, w_query, w_key, value_weight, lengths):
    block_rows = context.shape[0]
    normed = jnp.concatenate(
        [normalize(context, norm_gain), normalize(query_acts, norm_gain)], axis=0
    )

    def apply_weight(whole_weight):
        return jnp.dot(normed, whole_weight, preferred_element_type=jnp.float32).astype(
            jnp.bfloat16
        )

    whole_q, whole_k, whole_v = (
        lax.all_gather(w_query, "inner", axis=0, tiled=True),
        lax.all_gather(w_key, "inner", axis=0, tiled=True),
        lax.all_gather(value_weight, "inner", axis=0, tiled=True),
    )
    projected_k = apply_weight(whole_k)
    projected_v = apply_weight(whole_v)
    anchor = share_anchor(jnp.stack([projected_k[:block_rows], projected_v[:block_rows]]))
    projected_q = apply_weight(whole_q)
    position = lax.axis_index(("outer", "inner"))
    own_length = lengths[position]
    anchor_length = lengths[0]
    places = jnp.arange(block_rows, dtype=jnp.int32)
    causal = places[:, None] >= places[None, :]
    block_q = projected_q[:block_rows]
    block_k = projected_k[:block_rows]
    block_v = projected_v[:block_rows]
    query_q = projected_q[block_rows:]
    query_k = projected_k[block_rows:]
    query_v = projected_v[block_rows:]
    query_count = query_q.shape[0]
    own_allowed = causal & (places[None, :] < own_length)
    anchor_allowed = jnp.broadcast_to(
        (places[None, :] < anchor_length) & (position > 0), (block_rows, block_rows)
    )
    allowed = jnp.concatenate([anchor_allowed, own_allowed], axis=1)
    key_row_block = jnp.concatenate([anchor[0], block_k], axis=0)
    value_rows = jnp.concatenate([anchor[1], block_v], axis=0)
    block_out = finish(attend_part(block_q, key_row_block, value_rows, allowed))
    reached = jnp.broadcast_to(places[None, :] < own_length, (query_count, block_rows))
    block_part = attend_part(query_q, block_k, block_v, reached)
    highest = lax.pmax(block_part[0], ("outer", "inner"))
    rescale = jnp.exp(block_part[0] - highest)
    summed_parts = lax.psum(
        (block_part[1] * rescale, block_part[2] * spread(rescale)), ("outer", "inner")
    )
    merged = (highest, summed_parts[0], summed_parts[1])
    query_places = jnp.arange(query_count, dtype=jnp.int32)
    self_part = attend_part(
        query_q, query_k, query_v, query_places[:, None] >= query_places[None, :]
    )
    return (block_out, finish(combine(merged, self_part)))


def solution(mesh):
    in_specs = (
        P(("outer", "inner"), None),
        P(),
        P(),
        P("inner", None),
        P("inner", None),
        P("inner", None),
        P(),
    )
    out_specs = (P(("outer", "inner"), None), P())
    return jax.shard_map(
        per_device, mesh=mesh, in_specs=in_specs, out_specs=out_specs, check_vma=False
    )
```

profile of v0, /device:TPU:2, one launch (start us, length us, event | category | flops | bytes accessed | tf_op | source)
XLA Modules:
  0.0 875.9 jit_solution(4082930749184454192)
XLA Ops:
  7.2 0.7 all-gather.4.cloned.1.call-update
  8.0 0.7 all-gather.6.cloned.1.call-update
  8.7 1.2 fusion.9
  10.0 1.5 fusion
  11.5 0.9 fusion.11
  12.8 51.5 %all-gather.4.cloned.1.call-done = bf16[4096,512]{1,0:T(8,128)(2,1)} async-done(((bf16[128,512]{1,0:T(8,128)(2,1)}), bf16[4096,512]{1,0:T(8,128)(2,1)}) %all-gather.4.cloned.1.call-update) | async-done | bytes 4194320 | tf_op jit(solution)/shard_map/all_gather | solution.py:86
  64.3 3.2 convolution_convert_fusion.2
  67.6 49.9 %all-gather.6.cloned.1.call-done = bf16[4096,512]{1,0:T(8,128)(2,1)} async-done(((bf16[128,512]{1,0:T(8,128)(2,1)}), bf16[4096,512]{1,0:T(8,128)(2,1)}) %all-gather.6.cloned.1.call-update) | async-done | bytes 4194320 | tf_op jit(solution)/shard_map/all_gather | solution.py:87
  117.5 3.2 convolution_convert_fusion.1
  120.7 0.7 maximum_select_fusion
  124.1 0.8 copy.28
  124.9 0.7 concatenate.28
  126.2 0.6 reshape.109
  126.9 246.7 %all-reduce.3.cloned.1.call-done = bf16[2,128,512]{2,1,0:T(8,128)(2,1)} async-done(((bf16[2,128,512]{2,1,0:T(8,128)(2,1)}), bf16[2,128,512]{2,1,0:T(8,128)(2,1)}) %all-reduce.3.cloned.1.call-update) | async-done | bytes 262160 | tf_op jit(solution)/shard_map/psum | solution.py:14
  373.5 1.0 fusion.49
  374.6 0.8 copy.56
  375.4 76.8 %all-gather.8.cloned.1.call-done = bf16[4096,2048]{1,0:T(8,128)(2,1)} async-done(((bf16[128,2048]{1,0:T(8,128)(2,1)}), bf16[4096,2048]{1,0:T(8,128)(2,1)}) %all-gather.8.cloned.1.call-update) | async-done | bytes 16777232 | tf_op jit(solution)/shard_map/all_gather | solution.py:85
  452.2 7.7 convolution_convert_fusion
  463.1 76.0 %pmax.7 = f32[16,64]{1,0:T(8,128)S(1)} all-reduce(f32[16,64]{1,0:T(8,128)S(1)} %bitcast.97), channel_id=1, replica_groups=mesh['outer'=8,'inner'=32] {'outer','inner'}, use_global_device_ids=true, to_apply=%region_6.7 | all-reduce | flops 1024 | bytes 8192 | tf_op jit(solution)/shard_map/pmax | solution.py:115
  539.5 74.4 %psum.23 = f32[16,64]{1,0:T(8,128)S(1)} all-reduce(f32[16,64]{1,0:T(8,128)S(1)} %get-tuple-element.13), channel_id=1, replica_groups=mesh['outer'=8,'inner'=32] {'outer','inner'}, use_global_device_ids=true, to_apply=%region_10.11 | all-reduce | flops 1024 | bytes 8192 | tf_op jit(solution)/shard_map/psum | solution.py:117
  616.7 1.0 bitcast_multiply_fusion.2
  618.2 1.2 fusion.14
  619.3 247.2 %all-reduce.5.cloned.1.call-done = f32[64,2048]{1,0:T(8,128)} async-done(((f32[64,2048]{1,0:T(8,128)}), f32[64,2048]{1,0:T(8,128)}) %all-reduce.5.cloned.1.call-update) | async-done | bytes 524304 | tf_op jit(solution)/shard_map/psum | solution.py:117
  867.1 2.2 fusion.16
  (82 shorter events, 11.1 us)
Async XLA Ops:
  7.2 4.4 copy-start.1
  7.2 5.3 copy-start
  7.2 5.3 copy-start.10
  7.2 57.1 %all-gather.4.cloned.1.call-start = ((), (), s32[]{:S(2)}) async-start(), calls=%async_computation | async-start | bytes 4325376 | tf_op jit(solution)/shard_map/all_gather | solution.py:86
  7.9 109.5 %all-gather.6.cloned.1.call-start = ((), (), s32[]{:S(2)}) async-start(), calls=%async_computation.1 | async-start | bytes 4325376 | tf_op jit(solution)/shard_map/all_gather | solution.py:87
  8.7 364.9 %all-reduce.3.cloned.1.call-start = ((), (), s32[]{:S(2)}) async-start(), calls=%async_computation.2 | async-start | bytes 524288 | tf_op jit(solution)/shard_map/psum | solution.py:14
  12.5 105.0 %copy-start.3 = (bf16[64,4096]{1,0:T(8,128)(2,1)}, bf16[64,4096]{1,0:T(8,128)(2,1)S(1)}, u32[]{:S(2)}) copy-start(bf16[64,4096]{1,0:T(8,128)(2,1)S(1)} %fusion.11) | copy-start | bytes 1572868
  67.6 54.5 %copy-start.11 = (s32[256]{0:T(256)S(1)}, s32[256]{0:T(256)}, u32[]{:S(2)}) copy-start(s32[256]{0:T(256)} %param.13) | copy-start | bytes 3076
  120.6 331.5 %copy-start.4 = (bf16[64,4096]{1,0:T(8,128)(2,1)S(1)}, bf16[64,4096]{1,0:T(8,128)(2,1)}, u32[]{:S(2)}) copy-start(bf16[64,4096]{1,0:T(8,128)(2,1)} %copy-done.3) | copy-start | bytes 1572868
  121.4 330.7 %all-gather.8.cloned.1.call-start = ((), (), s32[]{:S(2)}) async-start(), calls=%async_computation.3 | async-start | bytes 17301504 | tf_op jit(solution)/shard_map/all_gather | solution.py:85
  122.0 744.5 %all-reduce.5.cloned.1.call-start = ((), (), s32[]{:S(2)}) async-start(), calls=%async_computation.4 | async-start | bytes 1048576 | tf_op jit(solution)/shard_map/psum | solution.py:117
  459.8 0.9 copy-start.2
  460.3 0.9 copy-start.5
  460.3 1.0 copy-start.6
  461.2 1.0 slice-start
  461.7 0.9 copy-start.9
  461.8 152.2 %copy-start.8 = (bf16[64,4,128]{2,1,0:T(4,128)(2,1)S(1)}, bf16[64,4,128]{2,1,0:T(4,128)(2,1)}, u32[]{:S(2)}) copy-start(bf16[64,4,128]{2,1,0:T(4,128)(2,1)} %reshape.106) | copy-start | bytes 196612
  462.1 152.5 %copy-start.7 = (bf16[64,4,128]{2,1,0:T(4,128)(2,1)S(1)}, bf16[64,4,128]{2,1,0:T(4,128)(2,1)}, u32[]{:S(2)}) copy-start(bf16[64,4,128]{2,1,0:T(4,128)(2,1)} %reshape.109) | copy-start | bytes 196612
Sparse Core Ops, SparseCore 0:
  10.6 53.7 all-gather.3
  66.9 50.5 all-gather.5
  123.5 250.0 all-reduce.2
  375.9 76.1 all-gather.7
  617.9 248.6 all-reduce.4
where the time goes:
time: 876 us
  waiting for transfers between devices  674 us (77%)
  blocking collectives  150 us (17%)
  matrix products  16.3 us (2%)
  between operations  14.2 us (2%)
  other arithmetic  11.4 us (1%)
  local copies, waits for them, and re-layouts  9.33 us (1%)
    psum x1, waiting for transfers between devices, per_device(): lax.psum((block_part[1] * rescale, block_part[2] * spread(rescale)), ('ou...  247 us
    psum x1, waiting for transfers between devices, broadcast(): return lax.psum(block, axis)  247 us
    all_gather x1, waiting for transfers between devices, per_device(): lax.all_gather(w_query, 'inner', axis=0, tiled=True)  76.8 us
    pmax x1, blocking collectives, per_device(): highest = lax.pmax(block_part[0], ('outer', 'inner'))  76 us
    psum x1, blocking collectives, per_device(): lax.psum((block_part[1] * rescale, block_part[2] * spread(rescale)), ('ou...  74.4 us
    all_gather x1, waiting for transfers between devices, per_device(): lax.all_gather(w_key, 'inner', axis=0, tiled=True)  51.5 us
    all_gather x1, waiting for transfers between devices, per_device(): lax.all_gather(value_weight, 'inner', axis=0, tiled=True)  49.9 us
  transfers between devices with their start and end apart: 5, of which 5 were waited for; matrix products, arithmetic and copies ran while one was open for 2% of the time, Pallas kernels for 0%

commit v1 on v0

--- a/solution.py
+++ b/solution.py
@@ -115,7 +115,7 @@
     highest = lax.pmax(block_part[0], ("outer", "inner"))
     rescale = jnp.exp(block_part[0] - highest)
     summed_parts = lax.psum(
-        (block_part[1] * rescale, block_part[2] * spread(rescale)), ("outer", "inner")
+        lax.psum((block_part[1] * rescale, block_part[2] * spread(rescale)), "inner"), "outer"
     )
     merged = (highest, summed_parts[0], summed_parts[1])
     query_places = jnp.arange(query_count, dtype=jnp.int32)

time: 876 us -> 815 us (0.930)
  waiting for transfers between devices: 674 us -> 612 us
    psum x1 -> x2, waiting for transfers between devices: 247 us -> 182 us  [the longest x1 110 us: per_device(): lax.psum((block_part[1] * rescale, block_part[2] * spread(rescale)), 'inn...]
    psum x1 -> x2, blocking collectives: 74.4 us -> 76.7 us  [the longest x1 60.3 us: per_device(): lax.psum((block_part[1] * rescale, block_part[2] * spread(rescale)), 'inn...]
  transfers between devices with their start and end apart: 5 -> 6, of which waited for: 5 -> 6; matrix products, arithmetic and copies ran while one was open for 2% -> 2% of each run, Pallas kernels for 0% -> 0%
where the time goes in v1:
time: 815 us; the launch traced here: 814 us
  waiting for transfers between devices  612 us (75%)
  blocking collectives  153 us (19%)
  matrix products  17.1 us (2%)
  between operations  14.5 us (2%)
  other arithmetic  11.5 us (1%)
    psum x1, waiting for transfers between devices, broadcast(): return lax.psum(block, axis)  249 us
    psum x1, waiting for transfers between devices, per_device(): lax.psum((block_part[1] * rescale, block_part[2] * spread(rescale)), 'inn...  110 us
    all_gather x1, waiting for transfers between devices, per_device(): lax.all_gather(w_query, 'inner', axis=0, tiled=True)  77.4 us
    pmax x1, blocking collectives, per_device(): highest = lax.pmax(block_part[0], ('outer', 'inner'))  76 us
    psum x1, waiting for transfers between devices, per_device(): lax.psum(lax.psum((block_part[1] * rescale, block_part[2] * spread(rescal...  72.1 us
    psum x1, blocking collectives, per_device(): lax.psum((block_part[1] * rescale, block_part[2] * spread(rescale)), 'inn...  60.3 us
    all_gather x1, waiting for transfers between devices, per_device(): lax.all_gather(w_key, 'inner', axis=0, tiled=True)  51.5 us
    all_gather x1, waiting for transfers between devices, per_device(): lax.all_gather(value_weight, 'inner', axis=0, tiled=True)  49.9 us
  transfers between devices with their start and end apart: 6, of which 6 were waited for; matrix products, arithmetic and copies ran while one was open for 2% of the time, Pallas kernels for 0%

profile of v1, /device:TPU:2, one launch (start us, length us, event | category | flops | bytes accessed | tf_op | source)
XLA Modules:
  0.0 814.2 jit_solution(17129923751523917955)
XLA Ops:
  7.2 0.7 all-gather.4.cloned.1.call-update
  8.0 0.7 all-gather.6.cloned.1.call-update
  8.7 1.2 fusion.9
  10.0 1.5 fusion
  11.5 0.9 fusion.11
  12.8 51.5 %all-gather.4.cloned.1.call-done = bf16[4096,512]{1,0:T(8,128)(2,1)} async-done(((bf16[128,512]{1,0:T(8,128)(2,1)}), bf16[4096,512]{1,0:T(8,128)(2,1)}) %all-gather.4.cloned.1.call-update) | async-done | bytes 4194320 | tf_op jit(solution)/shard_map/all_gather | solution.py:86
  64.3 3.2 convolution_convert_fusion.2
  67.6 49.9 %all-gather.6.cloned.1.call-done = bf16[4096,512]{1,0:T(8,128)(2,1)} async-done(((bf16[128,512]{1,0:T(8,128)(2,1)}), bf16[4096,512]{1,0:T(8,128)(2,1)}) %all-gather.6.cloned.1.call-update) | async-done | bytes 4194320 | tf_op jit(solution)/shard_map/all_gather | solution.py:87
  117.5 3.2 convolution_convert_fusion.1
  120.6 0.7 maximum_select_fusion
  122.7 0.7 compare_and_fusion
  124.5 249.0 %all-reduce.4.cloned.1.call-done = bf16[2,128,512]{2,1,0:T(8,128)(2,1)} async-done(((bf16[2,128,512]{2,1,0:T(8,128)(2,1)}), bf16[2,128,512]{2,1,0:T(8,128)(2,1)}) %all-reduce.4.cloned.1.call-update) | async-done | bytes 262160 | tf_op jit(solution)/shard_map/psum | solution.py:14
  373.5 1.0 fusion.49
  374.7 77.4 %all-gather.8.cloned.1.call-done = bf16[4096,2048]{1,0:T(8,128)(2,1)} async-done(((bf16[128,2048]{1,0:T(8,128)(2,1)}), bf16[4096,2048]{1,0:T(8,128)(2,1)}) %all-gather.8.cloned.1.call-update) | async-done | bytes 16777232 | tf_op jit(solution)/shard_map/all_gather | solution.py:85
  452.2 7.7 convolution_convert_fusion
  460.9 76.0 %pmax.7 = f32[16,64]{1,0:T(8,128)S(1)} all-reduce(f32[16,64]{1,0:T(8,128)S(1)} %bitcast.97), channel_id=1, replica_groups=mesh['outer'=8,'inner'=32] {'outer','inner'}, use_global_device_ids=true, to_apply=%region_6.7 | all-reduce | flops 1024 | bytes 8192 | tf_op jit(solution)/shard_map/pmax | solution.py:115
  537.3 60.3 %psum.38 = f32[16,64]{1,0:T(8,128)S(1)} all-reduce(f32[16,64]{1,0:T(8,128)S(1)} %get-tuple-element.13), channel_id=1, replica_groups=mesh['outer'=8,'inner'=32] {'inner'}, use_global_device_ids=true, to_apply=%region_11.12 | all-reduce | flops 1024 | bytes 8192 | tf_op jit(solution)/shard_map/psum | solution.py:118
  597.6 16.4 %psum.39 = f32[16,64]{1,0:T(8,128)S(1)} all-reduce(f32[16,64]{1,0:T(8,128)S(1)} %psum.38), channel_id=1, replica_groups=mesh['outer'=8,'inner'=32] {'outer'}, use_global_device_ids=true, to_apply=%region_12.13 | all-reduce | flops 1024 | bytes 8192 | tf_op jit(solution)/shard_map/psum | solution.py:117
  615.2 1.0 bitcast_multiply_fusion.2
  618.0 1.1 convolution_bitcast_fusion
  619.1 109.7 %all-reduce.6.cloned.1.call-done = f32[64,2048]{1,0:T(8,128)} async-done(((f32[64,2048]{1,0:T(8,128)}), f32[64,2048]{1,0:T(8,128)}) %all-reduce.6.cloned.1.call-update) | async-done | bytes 524304 | tf_op jit(solution)/shard_map/psum | solution.py:118
  731.2 1.2 fusion.14
  732.4 72.1 %all-reduce.8.cloned.1.call-done = f32[64,2048]{1,0:T(8,128)} async-done(((f32[64,2048]{1,0:T(8,128)}), f32[64,2048]{1,0:T(8,128)}) %all-reduce.8.cloned.1.call-update) | async-done | bytes 524304 | tf_op jit(solution)/shard_map/psum | solution.py:117
  805.1 2.2 fusion.16
  (71 shorter events, 10.3 us)
Async XLA Ops:
  7.2 4.4 copy-start.1
  7.2 5.3 copy-start
  7.2 5.3 copy-start.3
  7.2 57.1 %all-gather.4.cloned.1.call-start = ((), (), s32[]{:S(2)}) async-start(), calls=%async_computation | async-start | bytes 4325376 | tf_op jit(solution)/shard_map/all_gather | solution.py:86
  7.9 109.5 %all-gather.6.cloned.1.call-start = ((), (), s32[]{:S(2)}) async-start(), calls=%async_computation.1 | async-start | bytes 4325376 | tf_op jit(solution)/shard_map/all_gather | solution.py:87
  8.7 364.9 %all-reduce.4.cloned.1.call-start = ((), (), s32[]{:S(2)}) async-start(), calls=%async_computation.2 | async-start | bytes 524288 | tf_op jit(solution)/shard_map/psum | solution.py:14
  67.6 54.5 %copy-start.4 = (s32[256]{0:T(256)S(1)}, s32[256]{0:T(256)}, u32[]{:S(2)}) copy-start(s32[256]{0:T(256)} %param.13) | copy-start | bytes 3076
  121.4 330.7 %all-gather.8.cloned.1.call-start = ((), (), s32[]{:S(2)}) async-start(), calls=%async_computation.3 | async-start | bytes 17301504 | tf_op jit(solution)/shard_map/all_gather | solution.py:85
  122.0 606.8 %all-reduce.6.cloned.1.call-start = ((), (), s32[]{:S(2)}) async-start(), calls=%async_computation.4 | async-start | bytes 1048576 | tf_op jit(solution)/shard_map/psum | solution.py:118
  616.3 188.2 %all-reduce.8.cloned.1.call-start = ((), (), s32[]{:S(2)}) async-start(), calls=%async_computation.5 | async-start | bytes 1048576 | tf_op jit(solution)/shard_map/psum | solution.py:117
  729.1 1.0 copy-start.2
Sparse Core Ops, SparseCore 0:
  10.6 53.7 all-gather.3
  66.9 50.5 all-gather.5
  123.5 250.0 all-reduce.3
  376.0 76.1 all-gather.7
  616.4 112.3 all-reduce.5
  731.0 73.4 all-reduce.7
